TPU v7x, 32 devices: a whole 2x2x4 slice. The times are simulated.
32 devices in a mesh: src: 4 (over y, core), dst: 8 (over z, x).
Axes of the slice: x: 2, y: 2, z: 4, core: 2. Of those that a mesh axis runs over, the one named last changes fastest.
Arguments:
- features: bfloat16 [8192, 768], P(('src', 'dst')), may hold values from -6 to 6
- edge_tiles: bfloat16 [4, 8, 64, 128, 128], P('src', 'dst'), may hold values from -0.3125 to 0.3125
- tile_src: int32 [4, 8, 64], P('src', 'dst'), may hold values from 0 to 7
- tile_dst: int32 [4, 8, 64], P('src', 'dst'), may hold values from 0 to 15, as said below
- tile_count: int32 [4, 8], P('src', 'dst'), may hold values from 1 to 64, as said below
- weight: bfloat16 [768, 1024], replicated, may hold values from -0.21875 to 0.21875
- out_bias: float32 [1024], replicated, may hold values from -3 to 3
- out_grad: bfloat16 [8192, 1024], P(('src', 'dst')), may hold values from -6 to 6
Outputs:
- hidden: bfloat16 [8192, 1024], P(('src', 'dst'))
- feature_grad: bfloat16 [8192, 768], P(('src', 'dst'))
- weight_grad: float32 [768, 1024], replicated
- bias_grad: float32 [1024], replicated
Inputs may be any that keep to these rules, and one draw needn't show every extreme that they name: `tile_src`: block s of the source column of device (i, k) is block s % 2 of device (s // 2, k). `tile_dst`: block e of the destination row of device (i, k) is block e % 2 of device (i, e // 2). On one device, all tile slots whose destination blocks lie on one device name the same block. In every row of devices, slot 0 of every device names one common block. `tile_count`: some device uses all 64 slots.
All inputs are finite; a program needn't handle non-finite values.
Results may differ from a plain program's by a relative error of at most 0.024.
Values may be sent and summed in bfloat16 or wider, within the bound.
A program may use at most 128 MiB of HBM per device.

v0:
```python
import jax
import jax.numpy as jnp
from jax import lax
from jax.sharding import PartitionSpec as P


def per_device(features, edge_tiles, tile_src, tile_dst, tile_count, weight, out_bias, out_grad):
    capacity = edge_tiles.shape[2]
    edge_size = edge_tiles.shape[3]
    feat_width = features.shape[1]
    block_rows = features.shape[0]
    blocks = block_rows // edge_size
    masters = lax.axis_size("dst")
    holders = lax.axis_size("src")
    adjacency = edge_tiles.reshape(capacity, edge_size, edge_size)
    src_ids = tile_src.reshape(capacity)
    dst_ids = tile_dst.reshape(capacity)
    tile_total = tile_count.reshape(())
    alive_mask = jnp.arange(capacity, dtype=jnp.int32) < tile_total
    block_ids = jnp.arange(blocks, dtype=jnp.int32)
    owner_ids = dst_ids // blocks
    inner_ids = dst_ids % blocks
    column = lax.all_gather(features, "src", axis=0, tiled=True).reshape(
        holders * blocks, edge_size, feat_width
    )
    picked = column[src_ids]
    partial_value = jnp.einsum(
        "tij,tjf->tif", adjacency, picked, preferred_element_type=jnp.float32
    )
    routing = (owner_ids[None, :] == jnp.arange(masters, dtype=jnp.int32)[:, None]) & alive_mask[
        None, :
    ]
    outgoing = jnp.einsum("pt,tif->pif", routing.astype(jnp.float32), partial_value)
    wanted_block = jnp.max(jnp.where(routing, inner_ids[None, :], 0), axis=1)
    wanted_rows = jnp.broadcast_to(wanted_block[:, None], (masters, edge_size))
    incoming = lax.all_to_all(
        outgoing.astype(jnp.bfloat16), "dst", split_axis=0, concat_axis=0, tiled=True
    )
    asked = lax.all_to_all(wanted_rows, "dst", split_axis=0, concat_axis=0, tiled=True)
    chooser = (asked[None, :, :] == block_ids[:, None, None]).astype(jnp.bfloat16)
    aggregate = jnp.einsum(
        "jpr,prf->jrf", chooser, incoming, preferred_element_type=jnp.float32
    ).astype(jnp.bfloat16)
    preact = (
        jnp.einsum("jrf,fh->jrh", aggregate, weight, preferred_element_type=jnp.float32) + out_bias
    )
    aggregate, preact, asked = (aggregate, preact, asked)
    gate_value = jax.nn.sigmoid(preact)
    hidden = (preact * gate_value).astype(jnp.bfloat16).reshape(block_rows, -1)
    grad_in = out_grad.reshape(blocks, edge_size, -1).astype(jnp.float32)
    pre_grad = grad_in * (gate_value * (1.0 + preact * (1.0 - gate_value)))
    pre_grad_b = pre_grad.astype(jnp.bfloat16)
    weight_term = jnp.einsum(
        "jrf,jrh->fh", aggregate, pre_grad_b, preferred_element_type=jnp.float32
    )
    bias_term = jnp.sum(pre_grad, axis=(0, 1))
    weight_grad, bias_grad = lax.psum((weight_term, bias_term), ("src", "dst"))
    back = jnp.einsum("jrh,fh->jrf", pre_grad_b, weight, preferred_element_type=jnp.float32).astype(
        jnp.bfloat16
    )
    asked_block = asked[:, 0]
    selector = (asked_block[:, None] == block_ids[None, :]).astype(jnp.bfloat16)
    replies = jnp.einsum("pj,jrf->prf", selector, back, preferred_element_type=jnp.float32).astype(
        jnp.bfloat16
    )
    returned = lax.all_to_all(replies, "dst", split_axis=0, concat_axis=0, tiled=True)
    wanted = returned[owner_ids]
    source = jnp.einsum("tji,tjf->tif", adjacency, wanted, preferred_element_type=jnp.float32)
    src_routing = (
        src_ids[None, :] == jnp.arange(holders * blocks, dtype=jnp.int32)[:, None]
    ) & alive_mask[None, :]
    src_terms = jnp.einsum("kt,tif->kif", src_routing.astype(jnp.float32), source)
    summed = lax.psum_scatter(
        src_terms.reshape(holders * block_rows, feat_width).astype(jnp.bfloat16),
        "src",
        scatter_dimension=0,
        tiled=True,
    )
    return (hidden, summed, weight_grad, bias_grad)


def solution(mesh):
    in_specs = (
        P(("src", "dst"), None),
        P("src", "dst", None, None, None),
        P("src", "dst", None),
        P("src", "dst", None),
        P("src", "dst"),
        P(),
        P(),
        P(("src", "dst"), None),
    )
    out_specs = (P(("src", "dst"), None), P(("src", "dst"), None), P(), P())
    return jax.shard_map(
        per_device, mesh=mesh, in_specs=in_specs, out_specs=out_specs, check_vma=False
    )
```

profile of v0, /device:TPU:0, one launch (start us, length us, event | category | flops | bytes accessed | tf_op | source)
XLA Modules:
  0.0 330.1 jit_solution(10724298226550727925)
XLA Ops:
  10.0 7.3 %all-to-all-start.1 = ((s32[8,1,128]{2,1,0:T(1,128)}), s32[8,1,128]{2,1,0:T(1,128)S(1)}, u32[]{:S(2)}, u32[]{:S(2)}) async-start(s32[8,1,128]{2,1,0:T(1,128)} %broadcast_in_dim.16), calls=%async_computation.1 | async-start | bytes 8192 | tf_op jit(solution)/shard_map/all_to_all | solution.py:39
  18.0 14.0 %all-gather.2.cloned.1.call-done = bf16[1024,768]{1,0:T(8,128)(2,1)} async-done(((bf16[256,768]{1,0:T(8,128)(2,1)}), bf16[1024,768]{1,0:T(8,128)(2,1)}) %all-gather.2.cloned.1.call-update) | async-done | bytes 1572880 | tf_op jit(solution)/shard_map/all_gather | solution.py:23
  31.9 8.6 %gather_fusion = bf16[64,128,768]{2,1,0:T(8,128)(2,1)} fusion(bf16[8,128,768]{2,1,0:T(8,128)(2,1)} %bitcast.81, s32[1024]{0:T(1024)S(1)} %pad_clamp_fusion.1), kind=kCustom, calls=%fused_computation | custom fusion | bytes 25166080 | tf_op jit(solution)/shard_map/gather | solution.py:26
  40.6 9.1 %convolution_bitcast_fusion.1 = bf16[64,128,768]{1,2,0:T(8,128)(2,1)} fusion(bf16[64,128,768]{2,1,0:T(8,128)(2,1)} %gather_fusion, bf16[1,1,64,128,128]{4,3,2,1,0:T(8,128)(2,1)S(1)} %copy-done), kind=kOutput, calls=%fused_computation.3 | convolution fusion | flops 1610612736 | bytes 27262976 | tf_op jit(solution)/shard_map/tij,tjf->tif/dot_general | solution.py:27
  49.7 16.8 %copy.40 = bf16[64,128,768]{2,0,1:T(8,128)(2,1)} copy(bf16[64,128,768]{1,2,0:T(8,128)(2,1)} %convolution_bitcast_fusion.1) | data formatting | bytes 25165824 | tf_op jit(solution)/shard_map/tij,tjf->tif/dot_general | solution.py:27
  66.5 6.3 %convolution_convert_fusion.2 = bf16[8,128,768]{2,0,1:T(8,128)(2,1)S(1)} fusion(bf16[64,128,768]{2,0,1:T(8,128)(2,1)} %copy.40, s32[64]{0:T(128)S(1)} %get-tuple-element.8, pred[64]{0:T(512)(128)(4,1)S(1)} %iota_compare_fusion.2), kind=kOutput, calls=%fused_computation.9 | convolution fusion | flops 100664320 | bytes 14156096 | tf_op jit(solution)/shard_map/pt,tif->pif/dot_general | solution.py:33
  72.8 1.5 copy.41
  74.3 5.6 %all-to-all-start = ((bf16[8,128,768]{2,1,0:T(8,128)(2,1)}), bf16[8,128,768]{2,1,0:T(8,128)(2,1)}, u32[]{:S(2)}, u32[]{:S(2)}) async-start(bf16[8,128,768]{2,1,0:T(8,128)(2,1)} %copy.41), calls=%async_computation | async-start | bytes 3145728 | tf_op jit(solution)/shard_map/all_to_all | solution.py:36
  80.1 37.2 %all-to-all-done = bf16[8,128,768]{2,1,0:T(8,128)(2,1)} async-done(((bf16[8,128,768]{2,1,0:T(8,128)(2,1)}), bf16[8,128,768]{2,1,0:T(8,128)(2,1)}, u32[]{:S(2)}, u32[]{:S(2)}) %all-to-all-start) | async-done | bytes 1572896 | tf_op jit(solution)/shard_map/all_to_all | solution.py:36
  117.3 2.6 fusion.17
  120.3 3.3 %fusion.42 = (f32[1024]{0:T(1024)S(1)}, bf16[2,128,1024]{2,1,0:T(8,128)(2,1)S(1)}, bf16[2,128,1024]{2,1,0:T(8,128)(2,1)}) fusion(bf16[2,128,1024]{2,1,0:T(8,128)(2,1)S(1)} %bitcast.86, f32[1024]{0:T(1024)S(1)} %copy-done.4, bf16[2,128,768]{1,2,0:T(8,128)(2,1)S(1)} %copy.50, bf16[768,1024]{1,0:T(8,128)(2,1)} %param.13), kind=kOutput, calls=%fused_computation.63 | convolution fusion | flops 406322176 | bytes 3547136 | tf_op jit(solution)/shard_map/jrf,fh->jrh/dot_general | solution.py:45
  125.0 1.4 copy.46
  126.5 4.4 %all-to-all-start.2 = ((bf16[8,128,768]{2,1,0:T(8,128)(2,1)}), bf16[8,128,768]{2,1,0:T(8,128)(2,1)}, u32[]{:S(2)}, u32[]{:S(2)}) async-start(bf16[8,128,768]{2,1,0:T(8,128)(2,1)} %copy.46), calls=%async_computation.2 | async-start | bytes 3145728 | tf_op jit(solution)/shard_map/all_to_all | solution.py:66
  131.0 2.2 convolution_bitcast_fusion.2
  133.5 44.2 %all-to-all-done.2 = bf16[8,128,768]{2,1,0:T(8,128)(2,1)} async-done(((bf16[8,128,768]{2,1,0:T(8,128)(2,1)}), bf16[8,128,768]{2,1,0:T(8,128)(2,1)}, u32[]{:S(2)}, u32[]{:S(2)}) %all-to-all-start.2) | async-done | bytes 1572896 | tf_op jit(solution)/shard_map/all_to_all | solution.py:66
  177.7 8.6 %gather_fusion.1 = bf16[64,128,768]{2,1,0:T(8,128)(2,1)} fusion(bf16[8,128,768]{2,1,0:T(8,128)(2,1)} %all-to-all-done.2, s32[1024]{0:T(1024)S(1)} %pad_clamp_fusion), kind=kCustom, calls=%fused_computation.1 | custom fusion | bytes 25166080 | tf_op jit(solution)/shard_map/gather | solution.py:67
  186.4 9.3 %convolution_bitcast_fusion = bf16[64,128,768]{1,2,0:T(8,128)(2,1)} fusion(bf16[64,128,768]{2,1,0:T(8,128)(2,1)} %gather_fusion.1, bf16[1,1,64,128,128]{4,3,2,1,0:T(8,128)(2,1)S(1)} %copy-done), kind=kOutput, calls=%fused_computation.2 | convolution fusion | flops 1610612736 | bytes 27262976 | tf_op jit(solution)/shard_map/tji,tjf->tif/dot_general | solution.py:68
  195.6 16.8 %copy.48 = bf16[64,128,768]{2,0,1:T(8,128)(2,1)} copy(bf16[64,128,768]{1,2,0:T(8,128)(2,1)} %convolution_bitcast_fusion) | data formatting | bytes 25165824 | tf_op jit(solution)/shard_map/tji,tjf->tif/dot_general | solution.py:68
  212.5 6.3 %convolution_convert_fusion = bf16[8,128,768]{2,0,1:T(8,128)(2,1)S(1)} fusion(bf16[64,128,768]{2,0,1:T(8,128)(2,1)} %copy.48, s32[64]{0:T(128)S(1)} %bitcast.85, pred[64]{0:T(512)(128)(4,1)S(1)} %iota_compare_fusion.2), kind=kOutput, calls=%fused_computation.7 | convolution fusion | flops 100664320 | bytes 14156096 | tf_op jit(solution)/shard_map/kt,tif->kif/dot_general | solution.py:72
  218.8 1.5 copy.49
  220.3 38.3 %psum.15 = f32[1024]{0:T(1024)} all-reduce(f32[1024]{0:T(1024)S(1)} %get-tuple-element.4), channel_id=1, replica_groups=mesh['src'=4,'dst'=8] {'src','dst'}, use_global_device_ids=true, to_apply=%region_4.5 | all-reduce | flops 1024 | bytes 8192 | tf_op jit(solution)/shard_map/psum | solution.py:57
  258.7 31.1 %all-reduce.2.cloned.1.call-done = f32[768,1024]{1,0:T(8,128)} async-done(((f32[768,1024]{1,0:T(8,128)}), f32[768,1024]{1,0:T(8,128)}) %all-reduce.2.cloned.1.call-update) | async-done | bytes 3145744 | tf_op jit(solution)/shard_map/psum | solution.py:57
  289.7 29.9 %reduce-scatter.2.cloned.1.call-done = bf16[256,768]{1,0:T(8,128)(2,1)} async-done(((bf16[1024,768]{1,0:T(8,128)(2,1)}), bf16[256,768]{1,0:T(8,128)(2,1)}) %reduce-scatter.2.cloned.1.call-update) | async-done | bytes 393232 | tf_op jit(solution)/shard_map/reduce_scatter | solution.py:73
  319.6 4.0 %copy.63 = f32[768,1024]{1,0:T(8,128)} copy(f32[768,1024]{1,0:T(8,128)} %all-reduce.2.cloned.1.call-done) | data formatting | bytes 6291456
  (32 shorter events, 5.2 us)
Async XLA Ops:
  7.2 33.4 %copy-start = (bf16[1,1,64,128,128]{4,3,2,1,0:T(8,128)(2,1)S(1)}, bf16[1,1,64,128,128]{4,3,2,1,0:T(8,128)(2,1)}, u32[]{:S(2)}) copy-start(bf16[1,1,64,128,128]{4,3,2,1,0:T(8,128)(2,1)} %param.9) | copy-start | bytes 6291460
  7.2 24.8 %all-gather.2.cloned.1.call-start = ((), (), s32[]{:S(2)}) async-start(), calls=%async_computation.4 | async-start | bytes 1966080 | tf_op jit(solution)/shard_map/all_gather | solution.py:23
  10.0 64.2 %all-to-all-start.1 = ((s32[8,1,128]{2,1,0:T(1,128)}), s32[8,1,128]{2,1,0:T(1,128)S(1)}, u32[]{:S(2)}, u32[]{:S(2)}) async-start(s32[8,1,128]{2,1,0:T(1,128)} %broadcast_in_dim.16), calls=%async_computation.1 | async-start | bytes 8192 | tf_op jit(solution)/shard_map/all_to_all | solution.py:39
  74.3 43.0 %all-to-all-start = ((bf16[8,128,768]{2,1,0:T(8,128)(2,1)}), bf16[8,128,768]{2,1,0:T(8,128)(2,1)}, u32[]{:S(2)}, u32[]{:S(2)}) async-start(bf16[8,128,768]{2,1,0:T(8,128)(2,1)} %copy.41), calls=%async_computation | async-start | bytes 3145728 | tf_op jit(solution)/shard_map/all_to_all | solution.py:36
  79.8 40.5 %copy-start.3 = (bf16[256,1024]{1,0:T(8,128)(2,1)S(1)}, bf16[256,1024]{1,0:T(8,128)(2,1)}, u32[]{:S(2)}) copy-start(bf16[256,1024]{1,0:T(8,128)(2,1)} %param.15) | copy-start | bytes 1572868
  79.8 40.5 %copy-start.4 = (f32[1024]{0:T(1024)S(1)}, f32[1024]{0:T(1024)}, u32[]{:S(2)}) copy-start(f32[1024]{0:T(1024)} %param.14) | copy-start | bytes 12292
  120.3 3.3 %copy-start.2 = (bf16[768,1024]{1,0:T(8,128)(2,1)S(1)}, bf16[768,1024]{1,0:T(8,128)(2,1)}, u32[]{:S(2)}) copy-start(bf16[768,1024]{1,0:T(8,128)(2,1)} %param.13) | copy-start | bytes 4718596
  126.5 4.5 %copy-start.5 = (s32[1,1,64]{2,1,0:T(1,128)S(1)}, s32[1,1,64]{2,1,0:T(1,128)}, u32[]{:S(2)}) copy-start(s32[1,1,64]{2,1,0:T(1,128)} %param.11) | copy-start | bytes 772
  126.5 51.3 %all-to-all-start.2 = ((bf16[8,128,768]{2,1,0:T(8,128)(2,1)}), bf16[8,128,768]{2,1,0:T(8,128)(2,1)}, u32[]{:S(2)}, u32[]{:S(2)}) async-start(bf16[8,128,768]{2,1,0:T(8,128)(2,1)} %copy.46), calls=%async_computation.2 | async-start | bytes 3145728 | tf_op jit(solution)/shard_map/all_to_all | solution.py:66
  130.9 158.8 %all-reduce.2.cloned.1.call-start = ((), (), s32[]{:S(2)}) async-start(), calls=%async_computation.6 | async-start | bytes 6291456 | tf_op jit(solution)/shard_map/psum | solution.py:57
  133.3 186.4 %reduce-scatter.2.cloned.1.call-start = ((), (), s32[]{:S(2)}) async-start(), calls=%async_computation.5 | async-start | bytes 1966080 | tf_op jit(solution)/shard_map/reduce_scatter | solution.py:73
  195.6 16.8 %copy-start.1 = (s32[1,1,64]{2,1,0:T(1,128)S(1)}, s32[1,1,64]{2,1,0:T(1,128)}, u32[]{:S(2)}) copy-start(s32[1,1,64]{2,1,0:T(1,128)} %param.10) | copy-start | bytes 772
Sparse Core Ops, SparseCore 0:
  9.5 22.3 all-gather.1
  137.8 151.9 all-reduce.1
  292.8 26.7 reduce-scatter.1
where the time goes:
time: 331 us; the launch traced here: 330 us
  waiting for transfers between devices  157 us (47%)
  local copies, waits for them, and re-layouts  60.7 us (18%)
  matrix products  40.5 us (12%)
  blocking collectives  38.3 us (12%)
  starting transfers between devices  17.6 us (5%)
  between operations  14.5 us (4%)
    all_to_all x1, waiting for transfers between devices, per_device(): lax.all_to_all(replies, 'dst', split_axis=0, concat_axis=0, tiled=True)  44.2 us
    psum x1, blocking collectives, per_device(): weight_grad, bias_grad = lax.psum((weight_term, bias_term), ('src', 'dst'))  38.3 us
    all_to_all x1, waiting for transfers between devices, per_device(): lax.all_to_all(outgoing.astype(jnp.bfloat16), 'dst', split_axis=0, concat...  37.2 us
    psum x1, waiting for transfers between devices, per_device(): weight_grad, bias_grad = lax.psum((weight_term, bias_term), ('src', 'dst'))  31.1 us
    reduce_scatter x1, waiting for transfers between devices, per_device(): lax.psum_scatter(src_terms.reshape(holders * block_rows, feat_width).asty...  29.9 us
    dot_general x1, local copies, waits for them, and re-layouts, per_device(): jnp.einsum('tji,tjf->tif', adjacency, wanted, preferred_element_type=jnp....  16.8 us
    dot_general x1, local copies, waits for them, and re-layouts, per_device(): jnp.einsum('tij,tjf->tif', adjacency, picked, preferred_element_type=jnp....  16.8 us
    all_gather x1, waiting for transfers between devices, per_device(): lax.all_gather(features, 'src', axis=0, tiled=True)  14 us
  transfers between devices with their start and end apart: 6, of which 5 were waited for; matrix products, arithmetic and copies ran while one was open for 27% of the time, Pallas kernels for 0%

commit v1 on v0

--- a/solution.py
+++ b/solution.py
@@ -54,7 +54,7 @@
         "jrf,jrh->fh", aggregate, pre_grad_b, preferred_element_type=jnp.float32
     )
     bias_term = jnp.sum(pre_grad, axis=(0, 1))
-    weight_grad, bias_grad = lax.psum((weight_term, bias_term), ("src", "dst"))
+    weight_grad, bias_grad = lax.psum(lax.psum((weight_term, bias_term), "dst"), "src")
     back = jnp.einsum("jrh,fh->jrf", pre_grad_b, weight, preferred_element_type=jnp.float32).astype(
         jnp.bfloat16
     )

time: 331 us -> 398 us (1.20)
  waiting for transfers between devices: 157 us -> 234 us
  blocking collectives: 38.3 us -> 26.5 us
    psum x1 -> x2, waiting for transfers between devices: 31.1 us -> 85.6 us  [the longest x1 76.1 us: per_device(): lax.psum((weight_term, bias_term), 'dst')]
    all_to_all x1, waiting for transfers between devices: 44.2 us -> 65.4 us  [per_device(): lax.all_to_all(replies, 'dst', split_axis=0, concat_axis=0, tiled=True)]
    psum x1 -> x2, blocking collectives: 38.3 us -> 26.5 us  [the longest x1 19.5 us: per_device(): lax.psum((weight_term, bias_term), 'dst')]
  transfers between devices with their start and end apart: 6 -> 7, of which waited for: 5 -> 6; matrix products, arithmetic and copies ran while one was open for 27% -> 23% of each run, Pallas kernels for 0% -> 0%
where the time goes in v1:
time: 398 us; the launch traced here: 396 us
  waiting for transfers between devices  234 us (59%)
  local copies, waits for them, and re-layouts  60.5 us (15%)
  matrix products  41.8 us (11%)
  blocking collectives  26.5 us (7%)
  starting transfers between devices  17.6 us (4%)
  between operations  14.5 us (4%)
    psum x1, waiting for transfers between devices, per_device(): lax.psum((weight_term, bias_term), 'dst')  76.1 us
    all_to_all x1, waiting for transfers between devices, per_device(): lax.all_to_all(replies, 'dst', split_axis=0, concat_axis=0, tiled=True)  65.4 us
    all_to_all x1, waiting for transfers between devices, per_device(): lax.all_to_all(outgoing.astype(jnp.bfloat16), 'dst', split_axis=0, concat...  37.2 us
    reduce_scatter x1, waiting for transfers between devices, per_device(): lax.psum_scatter(src_terms.reshape(holders * block_rows, feat_width).asty...  31.2 us
    psum x1, blocking collectives, per_device(): lax.psum((weight_term, bias_term), 'dst')  19.5 us
    dot_general x1, local copies, waits for them, and re-layouts, per_device(): jnp.einsum('tji,tjf->tif', adjacency, wanted, preferred_element_type=jnp....  16.8 us
    dot_general x1, local copies, waits for them, and re-layouts, per_device(): jnp.einsum('tij,tjf->tif', adjacency, picked, preferred_element_type=jnp....  16.8 us
    all_gather x1, waiting for transfers between devices, per_device(): lax.all_gather(features, 'src', axis=0, tiled=True)  14 us
  transfers between devices with their start and end apart: 7, of which 6 were waited for; matrix products, arithmetic and copies ran while one was open for 23% of the time, Pallas kernels for 0%

profile of v1, /device:TPU:0, one launch (start us, length us, event | category | flops | bytes accessed | tf_op | source)
XLA Modules:
  0.0 396.5 jit_solution(8741359882224986218)
XLA Ops:
  10.0 7.3 %all-to-all-start.1 = ((s32[8,1,128]{2,1,0:T(1,128)}), s32[8,1,128]{2,1,0:T(1,128)S(1)}, u32[]{:S(2)}, u32[]{:S(2)}) async-start(s32[8,1,128]{2,1,0:T(1,128)} %broadcast_in_dim.16), calls=%async_computation.1 | async-start | bytes 8192 | tf_op jit(solution)/shard_map/all_to_all | solution.py:39
  18.0 14.0 %all-gather.2.cloned.1.call-done = bf16[1024,768]{1,0:T(8,128)(2,1)} async-done(((bf16[256,768]{1,0:T(8,128)(2,1)}), bf16[1024,768]{1,0:T(8,128)(2,1)}) %all-gather.2.cloned.1.call-update) | async-done | bytes 1572880 | tf_op jit(solution)/shard_map/all_gather | solution.py:23
  31.9 8.7 %gather_fusion = bf16[64,128,768]{2,1,0:T(8,128)(2,1)} fusion(bf16[8,128,768]{2,1,0:T(8,128)(2,1)} %bitcast.81, s32[1024]{0:T(1024)S(1)} %pad_clamp_fusion.1), kind=kCustom, calls=%fused_computation | custom fusion | bytes 25166080 | tf_op jit(solution)/shard_map/gather | solution.py:26
  40.6 9.1 %convolution_bitcast_fusion.1 = bf16[64,128,768]{1,2,0:T(8,128)(2,1)} fusion(bf16[64,128,768]{2,1,0:T(8,128)(2,1)} %gather_fusion, bf16[1,1,64,128,128]{4,3,2,1,0:T(8,128)(2,1)S(1)} %copy-done), kind=kOutput, calls=%fused_computation.3 | convolution fusion | flops 1610612736 | bytes 27262976 | tf_op jit(solution)/shard_map/tij,tjf->tif/dot_general | solution.py:27
  49.7 16.8 %copy.40 = bf16[64,128,768]{2,0,1:T(8,128)(2,1)} copy(bf16[64,128,768]{1,2,0:T(8,128)(2,1)} %convolution_bitcast_fusion.1) | data formatting | bytes 25165824 | tf_op jit(solution)/shard_map/tij,tjf->tif/dot_general | solution.py:27
  66.5 6.3 %convolution_convert_fusion.2 = bf16[8,128,768]{2,0,1:T(8,128)(2,1)S(1)} fusion(bf16[64,128,768]{2,0,1:T(8,128)(2,1)} %copy.40, s32[64]{0:T(128)S(1)} %get-tuple-element.8, pred[64]{0:T(512)(128)(4,1)S(1)} %iota_compare_fusion.2), kind=kOutput, calls=%fused_computation.9 | convolution fusion | flops 100664320 | bytes 14156096 | tf_op jit(solution)/shard_map/pt,tif->pif/dot_general | solution.py:33
  74.3 5.7 %all-to-all-start = ((bf16[8,128,768]{2,1,0:T(8,128)(2,1)}), bf16[8,128,768]{2,1,0:T(8,128)(2,1)}, u32[]{:S(2)}, u32[]{:S(2)}) async-start(bf16[8,128,768]{2,1,0:T(8,128)(2,1)} %copy.41), calls=%async_computation | async-start | bytes 3145728 | tf_op jit(solution)/shard_map/all_to_all | solution.py:36
  80.2 37.2 %all-to-all-done = bf16[8,128,768]{2,1,0:T(8,128)(2,1)} async-done(((bf16[8,128,768]{2,1,0:T(8,128)(2,1)}), bf16[8,128,768]{2,1,0:T(8,128)(2,1)}, u32[]{:S(2)}, u32[]{:S(2)}) %all-to-all-start) | async-done | bytes 1572896 | tf_op jit(solution)/shard_map/all_to_all | solution.py:36
  117.4 2.6 fusion.17
  120.5 3.2 fusion.42
  123.7 2.2 convolution_bitcast_fusion.2
  125.9 2.0 fusion.14
  130.1 4.3 %all-to-all-start.2 = ((bf16[8,128,768]{2,1,0:T(8,128)(2,1)}), bf16[8,128,768]{2,1,0:T(8,128)(2,1)}, u32[]{:S(2)}, u32[]{:S(2)}) async-start(bf16[8,128,768]{2,1,0:T(8,128)(2,1)} %copy.46), calls=%async_computation.2 | async-start | bytes 3145728 | tf_op jit(solution)/shard_map/all_to_all | solution.py:66
  134.7 65.4 %all-to-all-done.2 = bf16[8,128,768]{2,1,0:T(8,128)(2,1)} async-done(((bf16[8,128,768]{2,1,0:T(8,128)(2,1)}), bf16[8,128,768]{2,1,0:T(8,128)(2,1)}, u32[]{:S(2)}, u32[]{:S(2)}) %all-to-all-start.2) | async-done | bytes 1572896 | tf_op jit(solution)/shard_map/all_to_all | solution.py:66
  200.1 8.6 %gather_fusion.1 = bf16[64,128,768]{2,1,0:T(8,128)(2,1)} fusion(bf16[8,128,768]{2,1,0:T(8,128)(2,1)} %all-to-all-done.2, s32[1024]{0:T(1024)S(1)} %pad_clamp_fusion), kind=kCustom, calls=%fused_computation.1 | custom fusion | bytes 25166080 | tf_op jit(solution)/shard_map/gather | solution.py:67
  208.6 76.1 %all-reduce.3.cloned.1.call-done = f32[768,1024]{1,0:T(8,128)} async-done(((f32[768,1024]{1,0:T(8,128)}), f32[768,1024]{1,0:T(8,128)}) %all-reduce.3.cloned.1.call-update) | async-done | bytes 3145744 | tf_op jit(solution)/shard_map/psum | solution.py:57
  284.8 9.3 %convolution_bitcast_fusion = bf16[64,128,768]{1,2,0:T(8,128)(2,1)} fusion(bf16[64,128,768]{2,1,0:T(8,128)(2,1)} %gather_fusion.1, bf16[1,1,64,128,128]{4,3,2,1,0:T(8,128)(2,1)S(1)} %copy-done), kind=kOutput, calls=%fused_computation.2 | convolution fusion | flops 1610612736 | bytes 27262976 | tf_op jit(solution)/shard_map/tji,tjf->tif/dot_general | solution.py:68
  294.1 16.8 %copy.48 = bf16[64,128,768]{2,0,1:T(8,128)(2,1)} copy(bf16[64,128,768]{1,2,0:T(8,128)(2,1)} %convolution_bitcast_fusion) | data formatting | bytes 25165824 | tf_op jit(solution)/shard_map/tji,tjf->tif/dot_general | solution.py:68
  311.0 6.4 %convolution_convert_fusion = bf16[8,128,768]{2,0,1:T(8,128)(2,1)S(1)} fusion(bf16[64,128,768]{2,0,1:T(8,128)(2,1)} %copy.48, s32[64]{0:T(128)S(1)} %bitcast.85, pred[64]{0:T(512)(128)(4,1)S(1)} %iota_compare_fusion.2), kind=kOutput, calls=%fused_computation.7 | convolution fusion | flops 100664320 | bytes 14156096 | tf_op jit(solution)/shard_map/kt,tif->kif/dot_general | solution.py:72
  318.8 19.5 %psum.30 = f32[1024]{0:T(1024)S(1)} all-reduce(f32[1024]{0:T(1024)S(1)} %get-tuple-element.4), channel_id=1, replica_groups=mesh['src'=4,'dst'=8] {'dst'}, use_global_device_ids=true, to_apply=%region_5.6 | all-reduce | flops 1024 | bytes 8192 | tf_op jit(solution)/shard_map/psum | solution.py:57
  338.3 7.1 %psum.31 = f32[1024]{0:T(1024)} all-reduce(f32[1024]{0:T(1024)S(1)} %psum.30), channel_id=1, replica_groups=mesh['src'=4,'dst'=8] {'src'}, use_global_device_ids=true, to_apply=%region_6.7 | all-reduce | flops 1024 | bytes 8192 | tf_op jit(solution)/shard_map/psum | solution.py:57
  345.3 9.5 %all-reduce.5.cloned.1.call-done = f32[768,1024]{1,0:T(8,128)} async-done(((f32[768,1024]{1,0:T(8,128)}), f32[768,1024]{1,0:T(8,128)}) %all-reduce.5.cloned.1.call-update) | async-done | bytes 3145744 | tf_op jit(solution)/shard_map/psum | solution.py:57
  354.8 31.2 %reduce-scatter.2.cloned.1.call-done = bf16[256,768]{1,0:T(8,128)(2,1)} async-done(((bf16[1024,768]{1,0:T(8,128)(2,1)}), bf16[256,768]{1,0:T(8,128)(2,1)}) %reduce-scatter.2.cloned.1.call-update) | async-done | bytes 393232 | tf_op jit(solution)/shard_map/reduce_scatter | solution.py:73
  386.0 4.0 %copy.64 = f32[768,1024]{1,0:T(8,128)} copy(f32[768,1024]{1,0:T(8,128)} %all-reduce.5.cloned.1.call-done) | data formatting | bytes 6291456
  (34 shorter events, 9.0 us)
Async XLA Ops:
  7.2 33.4 %copy-start = (bf16[1,1,64,128,128]{4,3,2,1,0:T(8,128)(2,1)S(1)}, bf16[1,1,64,128,128]{4,3,2,1,0:T(8,128)(2,1)}, u32[]{:S(2)}) copy-start(bf16[1,1,64,128,128]{4,3,2,1,0:T(8,128)(2,1)} %param.9) | copy-start | bytes 6291460
  7.2 24.8 %all-gather.2.cloned.1.call-start = ((), (), s32[]{:S(2)}) async-start(), calls=%async_computation.4 | async-start | bytes 1966080 | tf_op jit(solution)/shard_map/all_gather | solution.py:23
  10.0 64.2 %all-to-all-start.1 = ((s32[8,1,128]{2,1,0:T(1,128)}), s32[8,1,128]{2,1,0:T(1,128)S(1)}, u32[]{:S(2)}, u32[]{:S(2)}) async-start(s32[8,1,128]{2,1,0:T(1,128)} %broadcast_in_dim.16), calls=%async_computation.1 | async-start | bytes 8192 | tf_op jit(solution)/shard_map/all_to_all | solution.py:39
  74.3 46.2 %copy-start.2 = (bf16[256,1024]{1,0:T(8,128)(2,1)S(1)}, bf16[256,1024]{1,0:T(8,128)(2,1)}, u32[]{:S(2)}) copy-start(bf16[256,1024]{1,0:T(8,128)(2,1)} %param.15) | copy-start | bytes 1572868
  74.3 46.2 %copy-start.3 = (f32[1024]{0:T(1024)S(1)}, f32[1024]{0:T(1024)}, u32[]{:S(2)}) copy-start(f32[1024]{0:T(1024)} %param.14) | copy-start | bytes 12292
  74.3 43.1 %all-to-all-start = ((bf16[8,128,768]{2,1,0:T(8,128)(2,1)}), bf16[8,128,768]{2,1,0:T(8,128)(2,1)}, u32[]{:S(2)}, u32[]{:S(2)}) async-start(bf16[8,128,768]{2,1,0:T(8,128)(2,1)} %copy.41), calls=%async_computation | async-start | bytes 3145728 | tf_op jit(solution)/shard_map/all_to_all | solution.py:36
  80.0 204.8 %all-reduce.3.cloned.1.call-start = ((), (), s32[]{:S(2)}) async-start(), calls=%async_computation.6 | async-start | bytes 6291456 | tf_op jit(solution)/shard_map/psum | solution.py:57
  128.7 6.0 %copy-start.4 = (s32[1,1,64]{2,1,0:T(1,128)S(1)}, s32[1,1,64]{2,1,0:T(1,128)}, u32[]{:S(2)}) copy-start(s32[1,1,64]{2,1,0:T(1,128)} %param.11) | copy-start | bytes 772
  130.1 70.0 %all-to-all-start.2 = ((bf16[8,128,768]{2,1,0:T(8,128)(2,1)}), bf16[8,128,768]{2,1,0:T(8,128)(2,1)}, u32[]{:S(2)}, u32[]{:S(2)}) async-start(bf16[8,128,768]{2,1,0:T(8,128)(2,1)} %copy.46), calls=%async_computation.2 | async-start | bytes 3145728 | tf_op jit(solution)/shard_map/all_to_all | solution.py:66
  134.4 220.4 %all-reduce.5.cloned.1.call-start = ((), (), s32[]{:S(2)}) async-start(), calls=%async_computation.7 | async-start | bytes 6291456 | tf_op jit(solution)/shard_map/psum | solution.py:57
  284.8 101.2 %reduce-scatter.2.cloned.1.call-start = ((), (), s32[]{:S(2)}) async-start(), calls=%async_computation.5 | async-start | bytes 1966080 | tf_op jit(solution)/shard_map/reduce_scatter | solution.py:73
  294.1 16.8 %copy-start.1 = (s32[1,1,64]{2,1,0:T(1,128)S(1)}, s32[1,1,64]{2,1,0:T(1,128)}, u32[]{:S(2)}) copy-start(s32[1,1,64]{2,1,0:T(1,128)} %param.10) | copy-start | bytes 772
Sparse Core Ops, SparseCore 0:
  9.5 22.3 all-gather.1
  126.0 158.6 all-reduce.2
  287.1 67.6 all-reduce.4
  357.8 28.1 reduce-scatter.1
